TPU v7x, 128 devices: a whole 4x4x4 slice. The times are simulated.
128 devices in a mesh: sec: 4 (over x), op: 32 (over z, y, core).
Axes of the slice: x: 4, y: 4, z: 4, core: 2. Of those that a mesh axis runs over, the one named last changes fastest.
Arguments:
- wavefunction: bfloat16 [4, 1024, 1024], P('sec'), may hold values from -6 to 6
- left_operator: bfloat16 [128, 4, 1024, 1024], P('op', 'sec'), may hold values from -0.011048543 to 0.35355339
- right_operator: bfloat16 [128, 1024, 1024], P('op'), may hold values from -0.125 to 1.125
- sector_size: int32 [4], replicated, may hold values from 512 to 1024
- term_shift: int32 [128], replicated, may hold values from 0 to 3, as said below
Outputs:
- sigma: float32 [4, 1024, 1024], P('sec', 'op')
- residual: float32 [4, 1024, 1024], P('sec', 'op')
Inputs may be any that keep to these rules, and one draw needn't show every extreme that they name: `term_shift`: among the 4 terms of one index of op (terms g * 4 to g * 4 + 3), the shifts are distinct.
All inputs are finite; a program needn't handle non-finite values.
Results may differ from a plain program's by a relative error of at most 0.0025.
Values may be sent and summed in bfloat16 or wider, within the bound.
A program may use at most 128 MiB of HBM per device.

v0:
```python
import jax
import jax.numpy as jnp
from jax import lax
from jax.sharding import Mesh
from jax.sharding import PartitionSpec as P

OP = ("op_0", "op_1", "op_2")
SEC_OP = ("sec", "op_0", "op_1", "op_2")


def over_axes(x, axes):
    for axis in axes:
        x = lax.psum(x, axis)
    return x


def per_device(wavefunction, left_operator, right_operator, sector_size, term_shift):
    sec_count = lax.axis_size("sec")
    op_count = lax.axis_size(OP)
    sec_index = lax.axis_index("sec")
    op_index = lax.axis_index(OP)
    term_count = left_operator.shape[0]
    sector_rows = wavefunction.shape[1]
    col_count = wavefunction.shape[2]
    row_count = sector_rows // op_count
    positions = jnp.arange(sector_rows, dtype=jnp.int32)
    own_size = sector_size[sec_index]
    masked = wavefunction[0] * (positions < own_size).astype(jnp.bfloat16)[:, None]
    left_image = jnp.einsum(
        "tmn,nk->tmk", left_operator[:, 0], masked, preferred_element_type=jnp.float32
    ).astype(jnp.bfloat16)
    right_image = jnp.einsum(
        "tmk,tkl->tml", left_image, right_operator, preferred_element_type=jnp.float32
    ).astype(jnp.bfloat16)
    local_shifts = lax.dynamic_slice_in_dim(term_shift, op_index * term_count, term_count)
    targets = (sec_index + local_shifts) % sec_count
    routing_onehot = (targets[:, None] == jnp.arange(sec_count, dtype=jnp.int32)[None, :]).astype(
        jnp.bfloat16
    )
    outgoing = jnp.einsum(
        "tn,tmk->nmk", routing_onehot, right_image, preferred_element_type=jnp.float32
    ).astype(jnp.bfloat16)
    blocks = outgoing.reshape(sec_count * op_count, row_count, col_count)
    incoming = lax.all_to_all(blocks, SEC_OP, split_axis=0, concat_axis=0, tiled=True)
    summed = jnp.sum(incoming, axis=0, dtype=jnp.float32)
    global_rows = op_index * row_count + jnp.arange(row_count, dtype=jnp.int32)
    out_mask = (global_rows < own_size).astype(jnp.float32)
    sigma_rows = summed * out_mask[:, None]
    state_rows = lax.dynamic_slice_in_dim(masked, op_index * row_count, row_count, 0).astype(
        jnp.float32
    )
    norm_sum, cross_sum = (
        over_axes(jnp.sum(state_rows * state_rows), SEC_OP),
        over_axes(jnp.sum(state_rows * sigma_rows), SEC_OP),
    )
    energy = cross_sum / norm_sum
    residual_rows = sigma_rows - energy * state_rows
    return (sigma_rows[None], residual_rows[None])


def solution(mesh):
    finer = Mesh(mesh.devices.reshape(mesh.shape["sec"], 4, 4, 2), ("sec", "op_0", "op_1", "op_2"))
    return jax.shard_map(
        per_device,
        mesh=finer,
        in_specs=(P("sec", None, None), P(OP, "sec", None, None), P(OP, None, None), P(), P()),
        out_specs=(P("sec", OP, None), P("sec", OP, None)),
        check_vma=False,
    )
```

profile of v0, /device:TPU:1, one launch (start us, length us, event | category | flops | bytes accessed | tf_op | source)
XLA Modules:
  0.0 231.8 jit_solution(6037880737334125754)
XLA Ops:
  0.6 1.2 dynamic_slice.10
  1.9 0.6 fusion.16
  2.5 12.7 %fusion.5 = bf16[1024,4,1024]{2,0,1:T(8,128)(2,1)S(1)} fusion(bf16[4,1,1024,1024]{3,2,1,0:T(8,128)(2,1)} %param.6, bf16[1,1024,1024]{2,1,0:T(8,128)(2,1)} %param.5, bf16[1024]{0:T(1024)(128)(2,1)S(1)} %fusion.16), kind=kOutput, calls=%fused_computation.8 | convolution fusion | flops 8598323200 | bytes 18876416 | tf_op jit(solution)/shard_map/tmn,nk->tmk/dot_general | solution.py:29
  15.2 0.0 copy-start
  15.2 22.8 %copy.19 = bf16[1024,4,1024]{2,1,0:T(4,128)(2,1)} copy(bf16[1024,4,1024]{2,0,1:T(8,128)(2,1)S(1)} %fusion.5) | data formatting | bytes 16777216
  38.0 0.0 copy-done
  38.0 0.1 and_select_fusion
  38.1 14.9 %fusion.3 = bf16[4,1024,1024]{2,1,0:T(8,128)(2,1)S(1)} fusion(bf16[4,1024,1024]{2,1,0:T(8,128)(2,1)} %param.7, bf16[4,1024,1024]{1,0,2:T(4,128)(2,1)} %bitcast.24), kind=kOutput, calls=%fused_computation.6 | convolution fusion | flops 8589934592 | bytes 25165824 | tf_op jit(solution)/shard_map/tmk,tkl->tml/dot_general | solution.py:32
  53.0 7.5 %fusion.8 = bf16[4,1024,1024]{2,0,1:T(4,128)(2,1)} fusion(bf16[4,1024,1024]{2,1,0:T(8,128)(2,1)S(1)} %fusion.3, s32[4]{0:T(128)S(1)} %and_select_fusion), kind=kOutput, calls=%fused_computation.9 | convolution fusion | flops 37748752 | bytes 16777232 | tf_op jit(solution)/shard_map/tn,tmk->nmk/dot_general | solution.py:40
  60.4 9.5 %copy.7 = bf16[4,1024,1024]{2,1,0:T(8,128)(2,1)} copy(bf16[4,1024,1024]{2,0,1:T(4,128)(2,1)} %fusion.8) | data formatting | bytes 16777216 | tf_op jit(solution)/shard_map/convert_element_type | solution.py:42
  69.9 12.0 %all-to-all-start = ((bf16[128,32,1024]{2,1,0:T(8,128)(2,1)}), bf16[128,32,1024]{2,1,0:T(8,128)(2,1)}, u32[]{:S(2)}, u32[]{:S(2)}) async-start(bf16[128,32,1024]{2,1,0:T(8,128)(2,1)} %bitcast.23), calls=%async_computation | async-start | bytes 16777216 | tf_op jit(solution)/shard_map/all_to_all | solution.py:44
  81.9 0.1 dynamic-slice
  81.9 0.6 compare_convert_fusion
  82.6 105.4 %all-to-all-done = bf16[128,32,1024]{2,1,0:T(8,128)(2,1)} async-done(((bf16[128,32,1024]{2,1,0:T(8,128)(2,1)}), bf16[128,32,1024]{2,1,0:T(8,128)(2,1)}, u32[]{:S(2)}, u32[]{:S(2)}) %all-to-all-start) | async-done | bytes 8388640 | tf_op jit(solution)/shard_map/all_to_all | solution.py:44
  188.0 5.2 %convert_reduce_fusion = f32[32,1024]{1,0:T(8,128)S(1)} fusion(bf16[128,32,1024]{2,1,0:T(8,128)(2,1)} %all-to-all-done), kind=kLoop, calls=%fused_computation.1 | loop fusion | flops 8355840 | bytes 8519680 | tf_op jit(solution)/shard_map/reduce_sum | solution.py:45
  193.2 0.7 bitcast_multiply_fusion
  194.0 1.6 fusion.13
  195.5 6.7 %all-reduce.2 = (f32[]{:T(128)}, f32[]{:T(128)}) all-reduce(f32[]{:T(128)} %get-tuple-element.3, f32[]{:T(128)} %get-tuple-element.2), channel_id=1, replica_groups=mesh['sec'=4,'op_0'=4,'op_1'=4,'op_2'=2] {'sec'}, use_global_device_ids=true, to_apply=%region_2.3 | all-reduce | flops 2 | bytes 16 | tf_op jit(solution)/shard_map/psum | solution.py:13
  202.2 7.9 %all-reduce.1 = (f32[]{:T(128)}, f32[]{:T(128)}) all-reduce(f32[]{:T(128)} %get-tuple-element.8, f32[]{:T(128)} %get-tuple-element.9), channel_id=1, replica_groups=mesh['sec'=4,'op_0'=4,'op_1'=4,'op_2'=2] {'op_0'}, use_global_device_ids=true, to_apply=%region_3.4 | all-reduce | flops 2 | bytes 16 | tf_op jit(solution)/shard_map/psum | solution.py:13
  210.1 9.3 %all-reduce = (f32[]{:T(128)}, f32[]{:T(128)}) all-reduce(f32[]{:T(128)} %get-tuple-element.6, f32[]{:T(128)} %get-tuple-element.7), channel_id=1, replica_groups=mesh['sec'=4,'op_0'=4,'op_1'=4,'op_2'=2] {'op_1'}, use_global_device_ids=true, to_apply=%region_4.5 | all-reduce | flops 2 | bytes 16 | tf_op jit(solution)/shard_map/psum | solution.py:13
  219.4 9.5 %all-reduce.3 = (f32[]{:T(128)}, f32[]{:T(128)}) all-reduce(f32[]{:T(128)} %get-tuple-element.4, f32[]{:T(128)} %get-tuple-element.5), channel_id=1, replica_groups=mesh['sec'=4,'op_0'=4,'op_1'=4,'op_2'=2] {'op_2'}, use_global_device_ids=true, to_apply=%region_5.6 | all-reduce | flops 2 | bytes 16 | tf_op jit(solution)/shard_map/psum | solution.py:13
  230.2 1.6 fusion.15
Async XLA Ops:
  15.2 22.8 %copy-start = (s32[128]{0:T(128)S(1)}, s32[128]{0:T(128)}, u32[]{:S(2)}) copy-start(s32[128]{0:T(128)} %param.9) | copy-start | bytes 1540
  69.9 118.1 %all-to-all-start = ((bf16[128,32,1024]{2,1,0:T(8,128)(2,1)}), bf16[128,32,1024]{2,1,0:T(8,128)(2,1)}, u32[]{:S(2)}, u32[]{:S(2)}) async-start(bf16[128,32,1024]{2,1,0:T(8,128)(2,1)} %bitcast.23), calls=%async_computation | async-start | bytes 16777216 | tf_op jit(solution)/shard_map/all_to_all | solution.py:44
where the time goes:
time: 232 us
  waiting for transfers between devices  105 us (45%)
  matrix products  35 us (15%)
  local copies, waits for them, and re-layouts  33.5 us (14%)
  blocking collectives  33.4 us (14%)
  starting transfers between devices  12 us (5%)
  other arithmetic  10.5 us (5%)
    all_to_all x1, waiting for transfers between devices, per_device(): lax.all_to_all(blocks, SEC_OP, split_axis=0, concat_axis=0, tiled=True)  105 us
    psum x4, blocking collectives, over_axes(): x = lax.psum(x, axis)  33.4 us
    unnamed x3, local copies, waits for them, and re-layouts  22.8 us
    dot_general x1, matrix products, per_device(): jnp.einsum('tmk,tkl->tml', left_image, right_operator, preferred_element_...  14.9 us
    dot_general x1, matrix products, per_device(): jnp.einsum('tmn,nk->tmk', left_operator[:, 0], masked, preferred_element_...  12.7 us
    all_to_all x1, starting transfers between devices, per_device(): lax.all_to_all(blocks, SEC_OP, split_axis=0, concat_axis=0, tiled=True)  12 us
    convert_element_type x1, local copies, waits for them, and re-layouts, per_device(): outgoing = jnp.einsum('tn,tmk->nmk', routing_onehot, right_image, preferr...  9.46 us
    dot_general x1, matrix products, per_device(): jnp.einsum('tn,tmk->nmk', routing_onehot, right_image, preferred_element_...  7.45 us
  transfers between devices with their start and end apart: 1, of which 1 were waited for; matrix products, arithmetic and copies ran while one was open for 0% of the time, Pallas kernels for 0%

commit v1 on v0

v1 whole, which is shorter than its diff:
```python
import jax
import jax.numpy as jnp
from jax import lax
from jax.experimental import pallas as pl
from jax.experimental.pallas import tpu as pltpu
from jax.sharding import Mesh
from jax.sharding import PartitionSpec as P

OP = ("op_0", "op_1", "op_2")
AXES = ("sec", "op_0", "op_1", "op_2")
MESH = pl.DeviceIdType.MESH
BF = jnp.bfloat16
F32 = jnp.float32
PAIRS = 8
ITEMS = 16
LAG = 4


def decode(p):
    own = lax.div(p, 6)
    far = 1 - own
    return far * lax.div(p, 3) + own * (p - 6), far * lax.rem(p, 3) + own * 3


def fold(v):
    v = jnp.sum(v.reshape(-1, 8, 256), axis=0)
    return v[:, :128] + v[:, 128:]


def kernel(
    shift, size, psi, psi_rows, left, right, sig_out, res_out,
    psib, left0, left1, right0, right1, image, rowsb,
    c_send, c_recv, sy, sz, ry, rz, ty, tz, rxy, rxz, toy, toz, uy, uz, ruy, ruz,
    acc, red, red_c, red_x, red_y, red_z,
    load_sem, send_sem, c_sem, y_sem, z_sem, xy_sem, xz_sem, uy_sem, uz_sem, red_send, red_recv,
):
    x, z, y, c = (lax.axis_index(a) for a in AXES)
    group = z * 8 + y * 2 + c
    live = size[x]

    def ring(me, d):
        return lax.rem(me + d, 4)

    leftb = (left0, left1)
    rightb = (right0, right1)
    psi_cp = pltpu.make_async_copy(psi, psib, load_sem.at[0])
    halves = (1 - c, c)
    left_cp = [
        [
            pltpu.make_async_copy(left.at[:, :, :, halves[f], b], leftb[b].at[:, f], load_sem.at[1 + 2 * b + f])
            for f in range(2)
        ]
        for b in range(2)
    ]
    right_cp = [
        pltpu.make_async_copy(right.at[:, :, pl.ds(h * 512, 512)], rightb[h], load_sem.at[5 + h]) for h in range(2)
    ]
    rows_cp = [
        pltpu.make_async_copy(
            psi_rows.at[:, :, c, b, :, pl.ds(h * 512, 512)], rowsb.at[b, h], load_sem.at[7 + 2 * b + h]
        )
        for b in range(2)
        for h in range(2)
    ]
    psi_cp.start()
    for cp in left_cp[0]:
        cp.start()
    for cp in right_cp:
        cp.start()
    for cp in left_cp[1] + rows_cp:
        cp.start()

    barrier = pltpu.get_barrier_semaphore()
    for d in range(1, 4):
        for axis, me in (("sec", x), ("op_0", z), ("op_1", y)):
            pl.semaphore_signal(barrier, inc=1, device_id={axis: ring(me, d)}, device_id_type=MESH)
    pl.semaphore_signal(barrier, inc=1, device_id={"op_2": 1 - c}, device_id_type=MESH)
    pl.semaphore_wait(barrier, 10)

    psi_cp.wait()

    @pl.loop(0, 4)
    def _(i):
        r = pl.multiple_of(512 + i * 128, 128)
        pos = lax.broadcasted_iota(jnp.int32, (128, 1024), 0) + r
        psib[pl.ds(r, 128), :] = jnp.where(pos < live, psib[pl.ds(r, 128), :].astype(F32), 0.0).astype(BF)

    def term_of(k):
        want = lax.rem(k + 1, 4)
        t = jnp.int32(0)
        for i in range(1, 4):
            t = jnp.where(shift[group * 4 + i] == want, i, t)
        return t

    def to(axis, where, src, dst, sem_s, sem_r):
        return pltpu.make_async_remote_copy(
            src_ref=src, dst_ref=dst, send_sem=sem_s, recv_sem=sem_r, device_id={axis: where}, device_id_type=MESH
        )

    def drain(ref, sem):
        pltpu.make_async_copy(ref, ref, sem).wait()

    def core_copy(n):
        return to("op_2", 1 - c, c_send.at[n], c_recv.at[n], send_sem.at[0], c_sem.at[n])

    def left_step(p, held):
        t = term_of(decode(p)[1])
        slot = lax.rem(p, 2)
        a = held[t].reshape(512, 1024)
        for q in range(4):
            cols = slice(q * 256, (q + 1) * 256)
            o = jnp.dot(a, psib[:, cols], preferred_element_type=F32).astype(BF)
            image[slot, :, :, cols] = o.reshape(2, 256, 256)

    def partner_half(p, h):
        t = term_of(decode(p)[1])
        n = p * 2 + h
        a = image[lax.rem(p, 2), 0]
        for q in range(2):
            cols = slice(q * 256, (q + 1) * 256)
            c_send[n, :, cols] = jnp.dot(a, rightb[h][t, :, cols], preferred_element_type=F32).astype(BF)
        core_copy(n).start()

    def own_half(p, h):
        b, k = decode(p)
        t = term_of(k)
        n = p * 2 + h
        core_copy(n).wait_recv()
        a = image[lax.rem(p, 2), 1]
        for q in range(2):
            cols = slice(q * 256, (q + 1) * 256)
            v = jnp.dot(a, rightb[h][t, :, cols], preferred_element_type=F32).astype(BF).astype(F32)
            v = (v + c_recv[n, :, cols].astype(F32)).astype(BF).reshape(4, 4, 16, 256)
            if q == 0:
                for i in range(4):
                    sy[n, i] = v[:, i]
            else:
                sz[n] = v
        for d in range(1, 4):
            to("op_1", ring(y, d), sy.at[n, ring(y, d)], ry.at[n, d - 1], send_sem.at[1], y_sem.at[n]).start()
            to("op_0", ring(z, d), sz.at[n, ring(z, d)], rz.at[n, d - 1], send_sem.at[2], z_sem.at[n]).start()

        @pl.when(k == 3)
        def _():
            part = jnp.zeros((8, 128), F32)
            for i in range(4):
                part += fold(sy[n, i].astype(F32) * rowsb[b, h, :, i, :, 0:256].astype(F32))
                part += fold(sz[n, i].astype(F32) * rowsb[b, h, i, :, :, 256:512].astype(F32))
            acc[0:8] += part

    def x_copies(g, k):
        who = ring(x, k + 1)
        return (
            to("sec", who, ty.at[g, k], rxy.at[g, k], send_sem.at[3], xy_sem.at[g]),
            to("sec", who, tz.at[g, k], rxz.at[g, k], send_sem.at[4], xz_sem.at[g]),
        )

    def second(n):
        b, k = decode(lax.div(n, 2))
        g = b * 2 + lax.rem(n, 2)
        drain(ry.at[n], y_sem.at[n])
        drain(rz.at[n], z_sem.at[n])
        vy = sy[n, y].astype(F32)
        vz = sz[n, z].astype(F32)
        for d in range(3):
            vy += ry[n, d].astype(F32)
            vz += rz[n, d].astype(F32)

        @pl.when(k < 3)
        def _():
            ty[g, k] = vy.astype(BF)
            tz[g, k] = vz.astype(BF)
            for cp in x_copies(g, k):
                cp.start()

        @pl.when(k == 3)
        def _():
            toy[g] = vy
            toz[g] = vz

    @pl.loop(0, PAIRS + 1)
    def _(p):
        @pl.when(p == 0)
        def _():
            acc[...] = jnp.zeros_like(acc)
            for cp in left_cp[0]:
                cp.wait()

        @pl.when(p == 3)
        def _():
            for cp in left_cp[1]:
                cp.wait()

        for b in range(2):

            @pl.when((p < PAIRS) & (decode(p)[0] == b))
            def _():
                left_step(p, leftb[b])

        @pl.when(p == 0)
        def _():
            right_cp[0].wait()

        @pl.when(p < PAIRS)
        def _():
            partner_half(p, 0)

        @pl.when(p >= 1)
        def _():
            own_half(p - 1, 1)

        @pl.when(p == 0)
        def _():
            right_cp[1].wait()

        @pl.when(p < PAIRS)
        def _():
            partner_half(p, 1)
            own_half(p, 0)

        @pl.when(p == 3)
        def _():
            for cp in rows_cp:
                cp.wait()
            for b in range(2):
                for h in range(2):
                    for i in range(4):
                        pos = (
                            lax.broadcasted_iota(jnp.int32, (4, 16, 512), 0) * 64
                            + lax.broadcasted_iota(jnp.int32, (4, 16, 512), 1)
                            + (i * 256 + c * 32 + b * 16)
                        )
                        rowsb[b, h, i] = jnp.where(pos < live, rowsb[b, h, i].astype(F32), 0.0).astype(BF)
            norm = jnp.zeros((8, 128), F32)
            for b in range(2):
                for h in range(2):
                    s = rowsb[b, h, z, y].astype(F32)
                    norm += fold(s[:, :256] * s[:, :256]) + fold(s[:, 256:] * s[:, 256:])
            acc[8:16] = norm

        for i in range(2):

            @pl.when((p * 2 + i >= LAG) & (p < PAIRS))
            def _():
                second(p * 2 + i - LAG)

    for g in range(4):
        b, h = divmod(g, 2)
        drain(rxy.at[g], xy_sem.at[g])
        drain(rxz.at[g], xz_sem.at[g])
        ay = rxy[g, 0].astype(F32) + rxy[g, 1].astype(F32) + rxy[g, 2].astype(F32)
        az = rxz[g, 0].astype(F32) + rxz[g, 1].astype(F32) + rxz[g, 2].astype(F32)
        acc[0:8] += fold(ay * rowsb[b, h, :, y, :, 0:256].astype(F32)) + fold(
            az * rowsb[b, h, z, :, :, 256:512].astype(F32)
        )

    def red_start(stage, axis, me, n, dst):
        for d in range(1, n):
            to(axis, lax.rem(me + d, n), red.at[stage], dst.at[d - 1], red_send.at[stage], red_recv.at[stage]).start()

    def red_finish(stage, n, dst):
        drain(dst, red_recv.at[stage])
        v = red[stage]
        for d in range(n - 1):
            v += dst[d]
        red[stage + 1] = v

    red[0] = acc[...]
    red_start(0, "op_2", c, 2, red_c)

    @pl.loop(ITEMS - LAG, ITEMS - 1)
    def _(n):
        second(n)

    red_finish(0, 2, red_c)
    red_start(1, "sec", x, 4, red_x)
    second(jnp.int32(ITEMS - 1))
    for g in range(4):
        vy = toy[g]
        vz = toz[g]
        for d in range(3):
            vy += rxy[g, d].astype(F32)
            vz += rxz[g, d].astype(F32)
        toy[g] = vy
        toz[g] = vz
        uy[g] = vy.astype(BF)
        uz[g] = vz.astype(BF)
        for d in range(1, 4):
            to("op_0", ring(z, d), uy.at[g, ring(z, d)], ruy.at[g, d - 1], send_sem.at[5], uy_sem.at[g]).start()
            to("op_1", ring(y, d), uz.at[g, ring(y, d)], ruz.at[g, d - 1], send_sem.at[6], uz_sem.at[g]).start()
    red_finish(1, 4, red_x)
    red_start(2, "op_1", y, 4, red_y)
    for g in range(4):
        b, h = divmod(g, 2)
        drain(ruy.at[g], uy_sem.at[g])
        drain(ruz.at[g], uz_sem.at[g])
        vy = toy[g, z]
        vz = toz[g, y]
        for d in range(3):
            vy += ruy[g, d].astype(F32)
            vz += ruz[g, d].astype(F32)
        first = z * 256 + y * 64 + c * 32 + b * 16
        keep = first + lax.broadcasted_iota(jnp.int32, (16, 256), 0) < live
        sig_out[b * 16 : b * 16 + 16, h * 512 : h * 512 + 256] = jnp.where(keep, vy, 0.0)
        sig_out[b * 16 : b * 16 + 16, h * 512 + 256 : h * 512 + 512] = jnp.where(keep, vz, 0.0)
    red_finish(2, 4, red_y)
    red_start(3, "op_0", z, 4, red_z)
    drain(red_z, red_recv.at[3])
    total = red[3] + red_z[0] + red_z[1] + red_z[2]
    energy = jnp.sum(total[0:8]) / jnp.sum(total[8:16])
    for b in range(2):
        for h in range(2):
            at = (slice(b * 16, b * 16 + 16), slice(h * 512, h * 512 + 512))
            res_out[at] = sig_out[at] - energy * rowsb[b, h, z, y].astype(F32)

    drain(c_send, send_sem.at[0])
    drain(ry, send_sem.at[1])
    drain(rz, send_sem.at[2])
    drain(ty, send_sem.at[3])
    drain(tz, send_sem.at[4])
    drain(ruy, send_sem.at[5])
    drain(ruz, send_sem.at[6])
    drain(red_c, red_send.at[0])
    drain(red_x, red_send.at[1])
    drain(red_y, red_send.at[2])
    drain(red_z, red_send.at[3])


def per_device(wavefunction, left_operator, right_operator, sector_size, term_shift):
    psi = wavefunction[0]
    hbm = pl.BlockSpec(memory_space=pl.ANY)
    smem = pl.BlockSpec(memory_space=pltpu.SMEM)
    vmem = pl.BlockSpec(memory_space=pltpu.VMEM)
    V = pltpu.VMEM
    DMA = pltpu.SemaphoreType.DMA
    out = jax.ShapeDtypeStruct((32, 1024), F32)
    sigma, residual = pl.pallas_call(
        kernel,
        out_shape=(out, out),
        in_specs=[smem, smem, hbm, hbm, hbm, hbm],
        out_specs=(vmem, vmem),
        scratch_shapes=[
            V((1024, 1024), BF),
            V((4, 2, 4, 4, 16, 1024), BF),
            V((4, 2, 4, 4, 16, 1024), BF),
            V((4, 1024, 512), BF),
            V((4, 1024, 512), BF),
            V((2, 2, 256, 1024), BF),
            V((2, 2, 4, 4, 16, 512), BF),
            V((ITEMS, 256, 512), BF),
            V((ITEMS, 256, 512), BF),
            V((ITEMS, 4, 4, 16, 256), BF),
            V((ITEMS, 4, 4, 16, 256), BF),
            V((ITEMS, 3, 4, 16, 256), BF),
            V((ITEMS, 3, 4, 16, 256), BF),
            V((4, 3, 4, 16, 256), BF),
            V((4, 3, 4, 16, 256), BF),
            V((4, 3, 4, 16, 256), BF),
            V((4, 3, 4, 16, 256), BF),
            V((4, 4, 16, 256), F32),
            V((4, 4, 16, 256), F32),
            V((4, 4, 16, 256), BF),
            V((4, 4, 16, 256), BF),
            V((4, 3, 16, 256), BF),
            V((4, 3, 16, 256), BF),
            V((16, 128), F32),
            V((4, 16, 128), F32),
            V((1, 16, 128), F32),
            V((3, 16, 128), F32),
            V((3, 16, 128), F32),
            V((3, 16, 128), F32),
            DMA((11,)),
            DMA((7,)),
            DMA((ITEMS,)),
            DMA((ITEMS,)),
            DMA((ITEMS,)),
            DMA((4,)),
            DMA((4,)),
            DMA((4,)),
            DMA((4,)),
            DMA((4,)),
            DMA((4,)),
        ],
        compiler_params=pltpu.CompilerParams(
            collective_id=0, has_side_effects=True, vmem_limit_bytes=60 * 2**20
        ),
        name="sigma_step",
    )(
        term_shift,
        sector_size,
        psi,
        psi.reshape(4, 4, 2, 2, 16, 1024),
        left_operator[:, 0].reshape(4, 4, 4, 2, 2, 16, 1024),
        right_operator,
    )
    return sigma[None], residual[None]


def solution(mesh):
    finer = Mesh(mesh.devices.reshape(mesh.shape["sec"], 4, 4, 2), AXES)
    return jax.shard_map(
        per_device,
        mesh=finer,
        in_specs=(P("sec", None, None), P(OP, "sec", None, None), P(OP, None, None), P(), P()),
        out_specs=(P("sec", OP, None), P("sec", OP, None)),
        check_vma=False,
    )
```

time: 232 us -> 58.9 us (0.25)
  waiting for transfers between devices: 105 us -> 0 us
  Pallas kernels: 0 us -> 54.2 us
  matrix products: 35 us -> 0 us
  blocking collectives: 33.4 us -> 0 us
  local copies, waits for them, and re-layouts: 33.5 us -> 3.14 us
  starting transfers between devices: 12 us -> 0 us
  other arithmetic: 10.5 us -> 0 us
    all_to_all x1 -> x0, waiting for transfers between devices: 105 us -> none  [per_device(): lax.all_to_all(blocks, SEC_OP, split_axis=0, concat_axis=0, tiled=True)]
    pallas_call x0 -> x1, Pallas kernels: none -> 54.2 us  [per_device(): pl.pallas_call(kernel, out_shape=(out, out), in_specs=[smem, smem, hbm, h...]
    dot_general x3 -> x0, matrix products: 35 us -> none  [the longest x1 14.9 us: per_device(): jnp.einsum('tmk,tkl->tml', left_image, right_operator, preferred_element_...]
    psum x4 -> x0, blocking collectives: 33.4 us -> none  [over_axes(): x = lax.psum(x, axis)]
    unnamed x3 -> x2, local copies, waits for them, and re-layouts: 22.8 us -> 3.14 us
    all_to_all x1 -> x0, starting transfers between devices: 12 us -> none  [per_device(): lax.all_to_all(blocks, SEC_OP, split_axis=0, concat_axis=0, tiled=True)]
    convert_element_type x1 -> x0, local copies, waits for them, and re-layouts: 9.46 us -> none  [per_device(): outgoing = jnp.einsum('tn,tmk->nmk', routing_onehot, right_image, preferr...]
    reduce_sum x2 -> x0, other arithmetic: 6.77 us -> none  [the longest x1 5.22 us: per_device(): summed = jnp.sum(incoming, axis=0, dtype=jnp.float32)]
  transfers between devices with their start and end apart: 1 -> 0, of which waited for: 1 -> 0; matrix products, arithmetic and copies ran while one was open for 0% -> 0% of each run, Pallas kernels for 0% -> 0%
where the time goes in v1:
time: 58.9 us; the launch traced here: 58 us
  Pallas kernels  54.2 us (92%)
  local copies, waits for them, and re-layouts  3.14 us (5%)
  between operations  0.64 us (1%)
    pallas_call x1, Pallas kernels, per_device(): pl.pallas_call(kernel, out_shape=(out, out), in_specs=[smem, smem, hbm, h...  54.2 us
    unnamed x2, local copies, waits for them, and re-layouts  3.14 us

profile of v1, /device:TPU:1, one launch (start us, length us, event | category | flops | bytes accessed | tf_op | source)
XLA Modules:
  0.0 58.0 jit_solution(9078097447112640020)
XLA Ops:
  0.6 54.2 %sigma_step.1 = (f32[32,1024]{1,0:T(8,128)}, f32[32,1024]{1,0:T(8,128)}) custom-call(s32[128]{0:T(128)} %shift.1, s32[4]{0:T(128)} %size.1, bf16[1024,1024]{1,0:T(8,128)(2,1)} %bitcast.6, bf16[4,4,2,2,16,1024]{5,4,3,2,1,0:T(8,128)(2,1)} %bitcast.7, bf16[4,4,4,2,2,16,1024]{6,5,4,3,2,1,0:T(8,128)(2,1)} %bitcast.5, bf16[4,1024,1024]{2,1,0:T(8,128)(2,1)} %right.1), custom_call_target="tpu_custom_call" | custom-call | tf_op jit(solution)/shard_map/sigma_step/pallas_call | solution.py:337
  54.9 1.6 %copy.9 = f32[1,32,1024]{2,1,0:T(8,128)} copy(f32[1,32,1024]{2,1,0:T(8,128)} %bitcast.9) | data formatting | bytes 262144
  56.4 1.6 %copy.10 = f32[1,32,1024]{2,1,0:T(8,128)} copy(f32[1,32,1024]{2,1,0:T(8,128)} %bitcast.8) | data formatting | bytes 262144

commit v2 on v0

v2 whole, which is shorter than its diff:
```python
import jax
import jax.numpy as jnp
from jax import lax
from jax.experimental import pallas as pl
from jax.experimental.pallas import tpu as pltpu
from jax.sharding import Mesh
from jax.sharding import PartitionSpec as P

OP = ("op_0", "op_1", "op_2")
AXES = ("sec", "op_0", "op_1", "op_2")
MESH = pl.DeviceIdType.MESH
BF = jnp.bfloat16
F32 = jnp.float32
PAIRS = 8
ITEMS = 16
LAG = 3


def decode(p):
    own = lax.div(p, 6)
    far = 1 - own
    return far * lax.div(p, 3) + own * (p - 6), far * lax.rem(p, 3) + own * 3


WX = 128
WY = (256, 128)
WZ = (128, 256)


def scratch():
    V = pltpu.VMEM
    DMA = pltpu.SemaphoreType.DMA
    out = {
        "psib": V((1024, 1024), BF),
        "image0": V((2, 256, 1024), BF),
        "image1": V((2, 256, 1024), BF),
        "rowsb": V((2, 2, 4, 4, 16, 512), BF),
        "c_send": V((ITEMS, 256, 512), BF),
        "c_recv": V((ITEMS, 256, 512), BF),
        "shift": pltpu.SMEM((128,), jnp.int32),
        "size": pltpu.SMEM((4,), jnp.int32),
        "sig": V((32, 1024), F32),
        "energy_row": V((1, 1024), F32),
        "unit_row": V((1, 1024), F32),
        "acc": V((16, 128), F32),
        "red": V((2, 8, 128), F32),
        "red_xy": V((15, 8, 128), F32),
        "red_zc": V((7, 8, 128), F32),
        "load_sem": DMA((13,)),
        "send_sem": DMA((20,)),
        "c_sem": DMA((ITEMS,)),
        "y_sem": DMA((ITEMS,)),
        "z_sem": DMA((ITEMS,)),
        "x_sem": DMA((4,)),
        "xy_sem": DMA((4,)),
        "xz_sem": DMA((4,)),
        "vx_sem": DMA((4,)),
        "ux_sem": DMA((4,)),
        "uy_sem": DMA((4,)),
        "uz_sem": DMA((4,)),
        "other_send": DMA((4,)),
        "other_recv": DMA((4,)),
        "red_send": DMA((2,)),
        "red_recv": DMA((2,)),
    }
    for h in range(2):
        out[f"left{h}"] = V((4, 2, 4, 4, 16, 1024), BF)
        out[f"right{h}"] = V((4, 1024, 512), BF)
        out[f"sx{h}"] = V((PAIRS, 4, 4, 16, WX), BF)
        out[f"rx{h}"] = V((2, 3, 4, 4, 16, WX), BF)
        out[f"vx{h}"] = V((2, 4, 4, 16, WX), BF)
        out[f"fx{h}"] = V((2, 4, 4, 16, WX), F32)
        out[f"rvx{h}"] = V((2, 3, 4, 16, WX), BF)
        out[f"gx{h}"] = V((2, 4, 16, WX), F32)
        out[f"ux{h}"] = V((2, 4, 16, WX), BF)
        out[f"rux{h}"] = V((2, 3, 16, WX), BF)
        for name, wide in (("y", WY[h]), ("z", WZ[h])):
            out[f"s{name}{h}"] = V((PAIRS, 4, 4, 16, wide), BF)
            out[f"r{name}{h}"] = V((PAIRS, 3, 4, 16, wide), BF)
            out[f"t{name}{h}"] = V((2, 3, 4, 16, wide), BF)
            out[f"rx{name}{h}"] = V((2, 3, 4, 16, wide), BF)
            out[f"to{name}{h}"] = V((2, 4, 16, wide), F32)
            out[f"u{name}{h}"] = V((2, 4, 16, wide), BF)
            out[f"ru{name}{h}"] = V((2, 3, 16, wide), BF)
            out[f"other{name}{h}"] = V((3, 4, 16, wide), BF)
    return out


def fold(v):
    wide = v.shape[-1]
    v = jnp.sum(v.reshape(-1, 8, wide), axis=0)
    return sum(v[:, i : i + 128] for i in range(0, wide, 128))


def kernel(shift_in, size_in, psi, psi_rows, left, right, sig_out, state_out, energy_out, unit_out, *held):
    ref = dict(zip(scratch(), held))

    def both(name):
        return ref[name + "0"], ref[name + "1"]

    psib, image0, image1, rowsb, c_send, c_recv, acc, red, red_xy, red_zc = (
        ref[name]
        for name in (
            "psib", "image0", "image1", "rowsb", "c_send", "c_recv", "acc", "red", "red_xy", "red_zc"
        )
    )
    sig, energy_row, unit_row = ref["sig"], ref["energy_row"], ref["unit_row"]
    load_sem, send_sem, c_sem, y_sem, z_sem, x_sem = (
        ref[name] for name in ("load_sem", "send_sem", "c_sem", "y_sem", "z_sem", "x_sem")
    )
    othery, otherz = both("othery"), both("otherz")
    other_send, other_recv = ref["other_send"], ref["other_recv"]
    xy_sem, xz_sem, vx_sem, ux_sem, uy_sem, uz_sem, red_send, red_recv = (
        ref[name]
        for name in ("xy_sem", "xz_sem", "vx_sem", "ux_sem", "uy_sem", "uz_sem", "red_send", "red_recv")
    )
    sx, rx, vx, fx, rvx, gx, ux, rux = (both(name) for name in ("sx", "rx", "vx", "fx", "rvx", "gx", "ux", "rux"))
    sy, ry, ty, rxy, toy, uy, ruy = (both(name) for name in ("sy", "ry", "ty", "rxy", "toy", "uy", "ruy"))
    sz, rz, tz, rxz, toz, uz, ruz = (both(name) for name in ("sz", "rz", "tz", "rxz", "toz", "uz", "ruz"))
    x, z, y, c = (lax.axis_index(a) for a in AXES)
    group = z * 8 + y * 2 + c
    shift, size = ref["shift"], ref["size"]

    def ring(me, d):
        return lax.rem(me + d, 4)

    leftb = both("left")
    rightb = both("right")
    psi_cp = pltpu.make_async_copy(psi, psib, load_sem.at[0])
    halves = (1 - c, c)
    left_cp = [
        [
            pltpu.make_async_copy(left.at[:, :, :, halves[f], b], leftb[b].at[:, f], load_sem.at[1 + 2 * b + f])
            for f in range(2)
        ]
        for b in range(2)
    ]
    right_cp = [
        pltpu.make_async_copy(right.at[:, :, pl.ds(h * 512, 512)], rightb[h], load_sem.at[5 + h]) for h in range(2)
    ]
    rows_cp = [
        pltpu.make_async_copy(
            psi_rows.at[:, :, c, b, :, pl.ds(h * 512, 512)], rowsb.at[b, h], load_sem.at[7 + 2 * b + h]
        )
        for b in range(2)
        for h in range(2)
    ]
    scalar_cp = [
        pltpu.make_async_copy(size_in, size, load_sem.at[11]),
        pltpu.make_async_copy(shift_in, shift, load_sem.at[12]),
    ]
    psi_cp.start()
    for cp in scalar_cp + left_cp[0]:
        cp.start()

    barrier = pltpu.get_barrier_semaphore()
    for d in range(1, 4):
        for e in range(4):
            pl.semaphore_signal(
                barrier, inc=1, device_id={"sec": ring(x, d), "op_1": ring(y, e)}, device_id_type=MESH
            )
        pl.semaphore_signal(barrier, inc=1, device_id={"op_1": ring(y, d)}, device_id_type=MESH)
        pl.semaphore_signal(barrier, inc=1, device_id={"op_0": ring(z, d)}, device_id_type=MESH)
        pl.semaphore_signal(barrier, inc=1, device_id={"op_0": ring(z, d), "op_2": 1 - c}, device_id_type=MESH)
    pl.semaphore_signal(barrier, inc=1, device_id={"op_2": 1 - c}, device_id_type=MESH)

    for cp in scalar_cp:
        cp.wait()
    live = size[x]
    psi_cp.wait()
    right_cp[0].start()
    for i in range(4):
        at = slice(512 + i * 128, 640 + i * 128)
        pos = lax.broadcasted_iota(jnp.int32, (128, 1024), 0) + (512 + i * 128)
        psib[at, :] = jnp.where(pos < live, psib[at, :].astype(F32), 0.0).astype(BF)
    acc[...] = jnp.zeros_like(acc)

    def term_of(k):
        want = lax.rem(k + 1, 4)
        t = jnp.int32(0)
        for i in range(1, 4):
            t = jnp.where(shift[group * 4 + i] == want, i, t)
        return t

    def send(device, src, dst, sem_s, sem_r):
        return pltpu.make_async_remote_copy(
            src_ref=src, dst_ref=dst, send_sem=sem_s, recv_sem=sem_r, device_id=device, device_id_type=MESH
        )

    def to(axis, where, src, dst, sem_s, sem_r):
        return send({axis: where}, src, dst, sem_s, sem_r)

    def drain(ref, sem):
        pltpu.make_async_copy(ref, ref, sem).wait()

    def core_copy(n):
        return to("op_2", 1 - c, c_send.at[n], c_recv.at[n], send_sem.at[0], c_sem.at[n])

    def state(b, h):
        cut = WX + WY[h]
        return (
            lambda *at: rowsb[(b, h, *at, slice(None), slice(0, WX))].astype(F32),
            lambda *at: rowsb[(b, h, *at, slice(None), slice(WX, cut))].astype(F32),
            lambda *at: rowsb[(b, h, *at, slice(None), slice(cut, 512))].astype(F32),
        )

    every = slice(None)

    def left_step(p):
        b, k = decode(p)
        t = term_of(k)
        slot = lax.rem(p, 2)
        for i in range(2):

            @pl.when(b == i)
            def _():
                a = leftb[i][t].reshape(512, 1024)
                for q in range(4):
                    cols = slice(q * 256, (q + 1) * 256)
                    o = jnp.dot(a, psib[:, cols], preferred_element_type=F32).astype(BF)
                    image0[slot, :, cols] = o[:256]
                    image1[slot, :, cols] = o[256:]

    def partner_half(p, halves):
        t = term_of(decode(p)[1])
        a = image0[lax.rem(p, 2)]
        for h in halves:
            for q in range(2):
                cols = slice(q * 256, (q + 1) * 256)
                c_send[p * 2 + h, :, cols] = jnp.dot(
                    a, rightb[h][t, :, cols], preferred_element_type=F32
                ).astype(BF)
        for h in halves:
            core_copy(p * 2 + h).start()

    def own_half(p):
        b, k = decode(p)
        t = term_of(k)
        for h in range(2):
            core_copy(p * 2 + h).wait_recv()
        a = image1[lax.rem(p, 2)]
        for h in range(2):
            for q in range(2):
                cols = slice(q * 256, (q + 1) * 256)
                v = jnp.dot(a, rightb[h][t, :, cols], preferred_element_type=F32).astype(BF).astype(F32)
                v = (v + c_recv[p * 2 + h, :, cols].astype(F32)).astype(BF).reshape(4, 4, 16, 256)
                for j in range(2):
                    w = v[..., j * 128 : (j + 1) * 128]
                    at = q * 256 + j * 128
                    if at < WX:
                        for i in range(4):
                            sx[h][p, i] = w[:, i]
                    elif at < WX + WY[h]:
                        for i in range(4):
                            sy[h][p, i, :, :, at - WX : at - WX + 128] = w[:, i]
                    else:
                        sz[h][p, :, :, :, at - WX - WY[h] : at - WX - WY[h] + 128] = w
        for h in range(2):
            n = p * 2 + h
            for d in range(1, 4):
                yd = ring(y, d)
                zd = ring(z, d)
                to("op_1", yd, sy[h].at[p, yd], ry[h].at[p, d - 1], send_sem.at[4 + h], y_sem.at[n]).start()
                to("op_0", zd, sz[h].at[p, zd], rz[h].at[p, d - 1], send_sem.at[6 + h], z_sem.at[n]).start()

        @pl.when(k < 3)
        def _():
            for h in range(2):
                to(
                    "sec", ring(x, k + 1), sx[h].at[p], rx[h].at[b, k], send_sem.at[2 + h], x_sem.at[b * 2 + h]
                ).start()

        @pl.when(k == 3)
        def _():
            for h in range(2):
                own_target(p, b, h)

    def own_target(p, b, h):
        g = b * 2 + h
        ox, oy, oz = state(b, h)
        drain(rx[h].at[b], x_sem.at[g])
        part = jnp.zeros((8, 128), F32)
        for i in range(4):
            w = sx[h][p, i].astype(F32)
            for j in range(3):
                w += rx[h][b, j, i].astype(F32)
            fx[h][b, i] = w
            vx[h][b, i] = w.astype(BF)
            part += fold(w * ox(every, i))
        for d in range(1, 4):
            yd = ring(y, d)
            to("op_1", yd, vx[h].at[b, yd], rvx[h].at[b, d - 1], send_sem.at[8 + h], vx_sem.at[g]).start()
        for i in range(4):
            part += fold(sy[h][p, i].astype(F32) * oy(every, i))
            part += fold(sz[h][p, i].astype(F32) * oz(i, every))
        acc[0:8] += part

    def second(p):
        b, k = decode(p)
        for h in range(2):
            n = p * 2 + h
            g = b * 2 + h
            drain(ry[h].at[p], y_sem.at[n])
            drain(rz[h].at[p], z_sem.at[n])
            vy = sy[h][p, y].astype(F32)
            vz = sz[h][p, z].astype(F32)
            for d in range(3):
                vy += ry[h][p, d].astype(F32)
                vz += rz[h][p, d].astype(F32)

            toy[h][b] = vy
            toz[h][b] = vz

            @pl.when(k < 3)
            def _():
                ty[h][b, k] = vy.astype(BF)
                tz[h][b, k] = vz.astype(BF)
                who = ring(x, k + 1)
                to("sec", who, ty[h].at[b, k], rxy[h].at[b, k], send_sem.at[10 + h], xy_sem.at[g]).start()
                to("sec", who, tz[h].at[b, k], rxz[h].at[b, k], send_sem.at[12 + h], xz_sem.at[g]).start()

    def cross_share(p):
        b, k = decode(p)
        there = size[ring(x, k + 1)]

        def row(outer, inner):
            return (
                lax.broadcasted_iota(jnp.int32, (4, 16, 128), 0) * outer
                + lax.broadcasted_iota(jnp.int32, (4, 16, 128), 1)
                + (inner + c * 32 + b * 16)
            )

        live_y = row(256, y * 64) < there
        live_z = row(64, z * 256) < there
        part = jnp.zeros((8, 128), F32)
        for h in range(2):
            for i in range(0, WY[h], 128):
                w = othery[h][k, :, :, i : i + 128].astype(F32)
                part += fold(ty[h][b, k, :, :, i : i + 128].astype(F32) * jnp.where(live_y, w, 0.0))
            for i in range(0, WZ[h], 128):
                w = otherz[h][k, :, :, i : i + 128].astype(F32)
                part += fold(tz[h][b, k, :, :, i : i + 128].astype(F32) * jnp.where(live_z, w, 0.0))
        acc[0:8] += part

    def mask_rows():
        for cp in rows_cp:
            cp.wait()
        for b in range(2):
            for h in range(2):
                for i in range(4):
                    pos = (
                        lax.broadcasted_iota(jnp.int32, (4, 16, 512), 0) * 64
                        + lax.broadcasted_iota(jnp.int32, (4, 16, 512), 1)
                        + (i * 256 + c * 32 + b * 16)
                    )
                    rowsb[b, h, i] = jnp.where(pos < live, rowsb[b, h, i].astype(F32), 0.0).astype(BF)
        norm = jnp.zeros((8, 128), F32)
        for b in range(2):
            for h in range(2):
                s = rowsb[b, h, z, y].astype(F32)
                norm += fold(s[:, :256] * s[:, :256]) + fold(s[:, 256:] * s[:, 256:])
        acc[8:16] = norm

    for cp in left_cp[0]:
        cp.wait()
    for cp in right_cp[1:] + left_cp[1] + rows_cp:
        cp.start()
    left_step(jnp.int32(0))
    pl.semaphore_wait(barrier, 22)
    for k in range(3):
        who = ring(x, 3 - k)
        for h in range(2):
            cols_y = pl.ds(h * 512 + WX, WY[h])
            cols_z = pl.ds(h * 512 + WX + WY[h], WZ[h])
            to("sec", who, psi_rows.at[:, y, c, 1, :, cols_y], othery[h].at[k], other_send.at[h], other_recv.at[h]).start()
            to("sec", who, psi_rows.at[z, :, c, 1, :, cols_z], otherz[h].at[k], other_send.at[2 + h], other_recv.at[2 + h]).start()
    right_cp[0].wait()
    partner_half(jnp.int32(0), (0,))
    left_step(jnp.int32(1))
    right_cp[1].wait()
    partner_half(jnp.int32(0), (1,))
    mask_rows()

    @pl.loop(1, PAIRS)
    def _(p):
        @pl.when(p == 2)
        def _():
            for cp in left_cp[1]:
                cp.wait()

        partner_half(p, (0, 1))
        own_half(p - 1)

        @pl.when(p < PAIRS - 1)
        def _():
            left_step(p + 1)

        @pl.when(p >= LAG)
        def _():
            second(p - LAG)

    for h in range(2):
        _, oy, oz = state(0, h)
        drain(rxy[h].at[0], xy_sem.at[h])
        drain(rxz[h].at[0], xz_sem.at[h])
        ay = rxy[h][0, 0].astype(F32) + rxy[h][0, 1].astype(F32) + rxy[h][0, 2].astype(F32)
        az = rxz[h][0, 0].astype(F32) + rxz[h][0, 1].astype(F32) + rxz[h][0, 2].astype(F32)
        acc[0:8] += fold(ay * oy(every, y)) + fold(az * oz(z, every))
        drain(othery[h], other_recv.at[h])
        drain(otherz[h], other_recv.at[2 + h])
    cross_share(jnp.int32(3))
    cross_share(jnp.int32(4))
    own_half(jnp.int32(PAIRS - 1))
    second(jnp.int32(5))
    cross_share(jnp.int32(5))
    groups = [(b, h) for b in range(2) for h in range(2)]

    def reduce_start(stage, dst, devices):
        for i, device in enumerate(devices):
            send(device, red.at[stage], dst.at[i], red_send.at[stage], red_recv.at[stage]).start()

    def reduce_finish(stage, dst, count):
        drain(dst, red_recv.at[stage])
        v = red[stage]
        for i in range(count):
            v += dst[i]
        return v

    unit_row[...] = jnp.ones_like(unit_row)
    state_cp = [
        pltpu.make_async_copy(
            rowsb.at[b, h, z, y],
            state_out.at[pl.ds(b * 16, 16), pl.ds(h * 512, 512)],
            load_sem.at[2 + b * 2 + h],
        )
        for b, h in groups
    ] + [pltpu.make_async_copy(unit_row, unit_out, load_sem.at[6])]
    for cp in state_cp:
        cp.start()

    red[0] = jnp.concatenate([acc[0:4] + acc[4:8], acc[8:12] + acc[12:16]], axis=0)
    plane = [{"sec": ring(x, i // 4), "op_1": ring(y, i % 4)} for i in range(1, 16)]
    reduce_start(0, red_xy, plane)

    for b in range(2):
        second(jnp.int32(PAIRS - 2 + b))
        for h in range(2):
            g = b * 2 + h
            if b == 1:
                drain(rxy[h].at[b], xy_sem.at[g])
                drain(rxz[h].at[b], xz_sem.at[g])
            vy = toy[h][b]
            vz = toz[h][b]
            for d in range(3):
                vy += rxy[h][b, d].astype(F32)
                vz += rxz[h][b, d].astype(F32)
            toy[h][b] = vy
            toz[h][b] = vz
            uy[h][b] = vy.astype(BF)
            uz[h][b] = vz.astype(BF)
            for d in range(1, 4):
                zd = ring(z, d)
                yd = ring(y, d)
                to("op_0", zd, uy[h].at[b, zd], ruy[h].at[b, d - 1], send_sem.at[14 + h], uy_sem.at[g]).start()
                to("op_1", yd, uz[h].at[b, yd], ruz[h].at[b, d - 1], send_sem.at[16 + h], uz_sem.at[g]).start()
            drain(rvx[h].at[b], vx_sem.at[g])
            v = fx[h][b, y]
            for d in range(3):
                v += rvx[h][b, d].astype(F32)
            gx[h][b] = v
            ux[h][b] = v.astype(BF)
            for d in range(1, 4):
                zd = ring(z, d)
                to("op_0", zd, ux[h].at[b, zd], rux[h].at[b, d - 1], send_sem.at[18 + h], ux_sem.at[g]).start()
    red[1] = reduce_finish(0, red_xy, 15)
    stack = [{"op_0": ring(z, i // 2), "op_2": lax.rem(c + i % 2, 2)} for i in range(1, 8)]
    reduce_start(1, red_zc, stack)
    for b, h in groups:
        g = b * 2 + h
        drain(ruy[h].at[b], uy_sem.at[g])
        drain(ruz[h].at[b], uz_sem.at[g])
        drain(rux[h].at[b], ux_sem.at[g])
        v = gx[h][b, z]
        vy = toy[h][b, z]
        vz = toz[h][b, y]
        for d in range(3):
            v += rux[h][b, d].astype(F32)
            vy += ruy[h][b, d].astype(F32)
            vz += ruz[h][b, d].astype(F32)
        first = z * 256 + y * 64 + c * 32 + b * 16
        rows = slice(b * 16, b * 16 + 16)
        at = h * 512
        cut = at + WX + WY[h]
        keep = (first + lax.broadcasted_iota(jnp.int32, (16, 512), 0)) < live
        sig[rows, at : at + WX] = jnp.where(keep[:, :WX], v, 0.0)
        sig[rows, at + WX : cut] = jnp.where(keep[:, WX : WX + WY[h]], vy, 0.0)
        sig[rows, cut : at + 512] = jnp.where(keep[:, WX + WY[h] :], vz, 0.0)
    sig_cp = pltpu.make_async_copy(sig, sig_out, load_sem.at[0])
    sig_cp.start()
    total = reduce_finish(1, red_zc, 7)
    energy = jnp.sum(total[0:4]) / jnp.sum(total[4:8])
    energy_row[...] = jnp.full((1, 1024), energy, F32)
    energy_cp = pltpu.make_async_copy(energy_row, energy_out, load_sem.at[1])
    energy_cp.start()

    drain(c_send, send_sem.at[0])
    for h in range(2):
        drain(othery[h], other_send.at[h])
        drain(otherz[h], other_send.at[2 + h])
        for i, buf in enumerate((rx, ry, rz, rvx, rxy, rxz, ruy, ruz, rux)):
            drain(buf[h], send_sem.at[2 + 2 * i + h])
    drain(red_xy, red_send.at[0])
    drain(red_zc, red_send.at[1])
    for cp in state_cp + [sig_cp, energy_cp]:
        cp.wait()


def per_device(wavefunction, left_operator, right_operator, sector_size, term_shift):
    psi = wavefunction[0]
    hbm = pl.BlockSpec(memory_space=pl.ANY)
    out = jax.ShapeDtypeStruct((32, 1024), F32)
    row = jax.ShapeDtypeStruct((1, 1024), F32)
    sigma, state, energy, unit = pl.pallas_call(
        kernel,
        out_shape=(out, jax.ShapeDtypeStruct((32, 1024), BF), row, row),
        in_specs=[hbm] * 6,
        out_specs=(hbm, hbm, hbm, hbm),
        scratch_shapes=list(scratch().values()),
        compiler_params=pltpu.CompilerParams(
            collective_id=0, has_side_effects=True, vmem_limit_bytes=60 * 2**20
        ),
        name="sigma_step",
    )(
        term_shift,
        sector_size,
        psi,
        psi.reshape(4, 4, 2, 2, 16, 1024),
        left_operator[:, 0].reshape(4, 4, 4, 2, 2, 16, 1024),
        right_operator,
    )
    sigma = sigma * unit
    return sigma[None], (sigma - energy * state.astype(F32))[None]


def solution(mesh):
    finer = Mesh(mesh.devices.reshape(mesh.shape["sec"], 4, 4, 2), AXES)
    return jax.shard_map(
        per_device,
        mesh=finer,
        in_specs=(P("sec", None, None), P(OP, "sec", None, None), P(OP, None, None), P(), P()),
        out_specs=(P("sec", OP, None), P("sec", OP, None)),
        check_vma=False,
    )
```

time: 232 us -> 50.9 us (0.22)
  waiting for transfers between devices: 105 us -> 0 us
  Pallas kernels: 0 us -> 48.5 us
  matrix products: 35 us -> 0 us
  local copies, waits for them, and re-layouts: 33.5 us -> 0 us
  blocking collectives: 33.4 us -> 0 us
  starting transfers between devices: 12 us -> 0 us
  other arithmetic: 10.5 us -> 1.63 us
    all_to_all x1 -> x0, waiting for transfers between devices: 105 us -> none  [per_device(): lax.all_to_all(blocks, SEC_OP, split_axis=0, concat_axis=0, tiled=True)]
    pallas_call x0 -> x1, Pallas kernels: none -> 48.5 us  [per_device(): pl.pallas_call(kernel, out_shape=(out, jax.ShapeDtypeStruct((32, 1024), B...]
    dot_general x3 -> x0, matrix products: 35 us -> none  [the longest x1 14.9 us: per_device(): jnp.einsum('tmk,tkl->tml', left_image, right_operator, preferred_element_...]
    psum x4 -> x0, blocking collectives: 33.4 us -> none  [over_axes(): x = lax.psum(x, axis)]
    unnamed x3 -> x0, local copies, waits for them, and re-layouts: 22.8 us -> none
    all_to_all x1 -> x0, starting transfers between devices: 12 us -> none  [per_device(): lax.all_to_all(blocks, SEC_OP, split_axis=0, concat_axis=0, tiled=True)]
    convert_element_type x1 -> x0, local copies, waits for them, and re-layouts: 9.46 us -> none  [per_device(): outgoing = jnp.einsum('tn,tmk->nmk', routing_onehot, right_image, preferr...]
    reduce_sum x2 -> x0, other arithmetic: 6.77 us -> none  [the longest x1 5.22 us: per_device(): summed = jnp.sum(incoming, axis=0, dtype=jnp.float32)]
  transfers between devices with their start and end apart: 1 -> 0, of which waited for: 1 -> 0; matrix products, arithmetic and copies ran while one was open for 0% -> 0% of each run, Pallas kernels for 0% -> 0%
where the time goes in v2:
time: 50.9 us; the launch traced here: 50.7 us
  Pallas kernels  48.5 us (95%)
  other arithmetic  1.63 us (3%)
  between operations  0.64 us (1%)
    pallas_call x1, Pallas kernels, per_device(): pl.pallas_call(kernel, out_shape=(out, jax.ShapeDtypeStruct((32, 1024), B...  48.5 us
    broadcast_in_dim x1, other arithmetic, per_device(): return (sigma[None], (sigma - energy * state.astype(F32))[None])  1.63 us

profile of v2, /device:TPU:1, one launch (start us, length us, event | category | flops | bytes accessed | tf_op | source)
XLA Modules:
  0.0 50.7 jit_solution(14189823286083399968)
XLA Ops:
  0.6 48.5 %sigma_step.1 = (f32[32,1024]{1,0:T(8,128)}, bf16[32,1024]{1,0:T(8,128)(2,1)}, f32[1,1024]{1,0:T(1,128)}, f32[1,1024]{1,0:T(1,128)}) custom-call(s32[128]{0:T(128)} %shift_in.1, s32[4]{0:T(128)} %size_in.1, bf16[1024,1024]{1,0:T(8,128)(2,1)} %bitcast.10, bf16[4,4,2,2,16,1024]{5,4,3,2,1,0:T(8,128)(2,1)} %bitcast.11, ...), custom_call_target="tpu_custom_call" | custom-call | tf_op jit(solution)/shard_map/sigma_step/pallas_call | solution.py:523
  49.1 1.6 %subtract_bitcast_fusion = (f32[1,32,1024]{2,1,0:T(8,128)}, f32[1,32,1024]{2,1,0:T(8,128)}) fusion(bf16[32,1024]{1,0:T(8,128)(2,1)} %get-tuple-element.9, f32[32,1024]{1,0:T(8,128)} %get-tuple-element.6, f32[1024]{0:T(1024)} %bitcast.12, f32[1024]{0:T(1024)} %bitcast.13), kind=kLoop, calls=%fused_computation | loop fusion | flops 131072 | bytes 466944 | tf_op jit(solution)/shard_map/broadcast_in_dim | solution.py:542

commit v3 on v2

--- a/solution.py
+++ b/solution.py
@@ -17,14 +17,12 @@
 
 
 def decode(p):
-    own = lax.div(p, 6)
-    far = 1 - own
-    return far * lax.div(p, 3) + own * (p - 6), far * lax.rem(p, 3) + own * 3
-
-
-WX = 128
-WY = (256, 128)
-WZ = (128, 256)
+    return (p // 3, p % 3) if p < 6 else (p - 6, 3)
+
+
+WX = (128, 0)
+WY = ((256, 128), (256, 256))
+WZ = ((128, 256), (256, 256))
 
 
 def scratch():
@@ -47,15 +45,15 @@
         "red_xy": V((15, 8, 128), F32),
         "red_zc": V((7, 8, 128), F32),
         "load_sem": DMA((13,)),
-        "send_sem": DMA((20,)),
+        "send_sem": DMA((32,)),
         "c_sem": DMA((ITEMS,)),
         "y_sem": DMA((ITEMS,)),
         "z_sem": DMA((ITEMS,)),
-        "x_sem": DMA((4,)),
+        "x_sem": DMA((2,)),
         "xy_sem": DMA((4,)),
         "xz_sem": DMA((4,)),
-        "vx_sem": DMA((4,)),
-        "ux_sem": DMA((4,)),
+        "vx_sem": DMA((2,)),
+        "ux_sem": DMA((2,)),
         "uy_sem": DMA((4,)),
         "uz_sem": DMA((4,)),
         "other_send": DMA((4,)),
@@ -66,23 +64,25 @@
     for h in range(2):
         out[f"left{h}"] = V((4, 2, 4, 4, 16, 1024), BF)
         out[f"right{h}"] = V((4, 1024, 512), BF)
-        out[f"sx{h}"] = V((PAIRS, 4, 4, 16, WX), BF)
-        out[f"rx{h}"] = V((2, 3, 4, 4, 16, WX), BF)
-        out[f"vx{h}"] = V((2, 4, 4, 16, WX), BF)
-        out[f"fx{h}"] = V((2, 4, 4, 16, WX), F32)
-        out[f"rvx{h}"] = V((2, 3, 4, 16, WX), BF)
-        out[f"gx{h}"] = V((2, 4, 16, WX), F32)
-        out[f"ux{h}"] = V((2, 4, 16, WX), BF)
-        out[f"rux{h}"] = V((2, 3, 16, WX), BF)
-        for name, wide in (("y", WY[h]), ("z", WZ[h])):
-            out[f"s{name}{h}"] = V((PAIRS, 4, 4, 16, wide), BF)
-            out[f"r{name}{h}"] = V((PAIRS, 3, 4, 16, wide), BF)
-            out[f"t{name}{h}"] = V((2, 3, 4, 16, wide), BF)
-            out[f"rx{name}{h}"] = V((2, 3, 4, 16, wide), BF)
-            out[f"to{name}{h}"] = V((2, 4, 16, wide), F32)
-            out[f"u{name}{h}"] = V((2, 4, 16, wide), BF)
-            out[f"ru{name}{h}"] = V((2, 3, 16, wide), BF)
-            out[f"other{name}{h}"] = V((3, 4, 16, wide), BF)
+        out[f"sx{h}"] = V((4, 4, 4, 16, WX[0]), BF)
+        out[f"rx{h}"] = V((3, 4, 4, 16, WX[0]), BF)
+        out[f"vx{h}"] = V((4, 4, 16, WX[0]), BF)
+        out[f"fx{h}"] = V((4, 4, 16, WX[0]), F32)
+        out[f"rvx{h}"] = V((3, 4, 16, WX[0]), BF)
+        out[f"gx{h}"] = V((4, 16, WX[0]), F32)
+        out[f"ux{h}"] = V((4, 16, WX[0]), BF)
+        out[f"rux{h}"] = V((3, 16, WX[0]), BF)
+        for name, widths in (("y", WY), ("z", WZ)):
+            out[f"other{name}{h}"] = V((3, 4, 16, widths[1][h]), BF)
+            for b in range(2):
+                wide = widths[b][h]
+                out[f"s{name}{b}{h}"] = V((4, 4, 4, 16, wide), BF)
+                out[f"r{name}{b}{h}"] = V((4, 3, 4, 16, wide), BF)
+                out[f"t{name}{b}{h}"] = V((3, 4, 16, wide), BF)
+                out[f"rx{name}{b}{h}"] = V((3, 4, 16, wide), BF)
+                out[f"to{name}{b}{h}"] = V((4, 16, wide), F32)
+                out[f"u{name}{b}{h}"] = V((4, 16, wide), BF)
+                out[f"ru{name}{b}{h}"] = V((3, 16, wide), BF)
     return out
 
 
@@ -97,6 +97,9 @@
 
     def both(name):
         return ref[name + "0"], ref[name + "1"]
+
+    def four(name):
+        return both(name + "0"), both(name + "1")
 
     psib, image0, image1, rowsb, c_send, c_recv, acc, red, red_xy, red_zc = (
         ref[name]
@@ -115,8 +118,8 @@
         for name in ("xy_sem", "xz_sem", "vx_sem", "ux_sem", "uy_sem", "uz_sem", "red_send", "red_recv")
     )
     sx, rx, vx, fx, rvx, gx, ux, rux = (both(name) for name in ("sx", "rx", "vx", "fx", "rvx", "gx", "ux", "rux"))
-    sy, ry, ty, rxy, toy, uy, ruy = (both(name) for name in ("sy", "ry", "ty", "rxy", "toy", "uy", "ruy"))
-    sz, rz, tz, rxz, toz, uz, ruz = (both(name) for name in ("sz", "rz", "tz", "rxz", "toz", "uz", "ruz"))
+    sy, ry, ty, rxy, toy, uy, ruy = (four(name) for name in ("sy", "ry", "ty", "rxy", "toy", "uy", "ruy"))
+    sz, rz, tz, rxz, toz, uz, ruz = (four(name) for name in ("sz", "rz", "tz", "rxz", "toz", "uz", "ruz"))
     x, z, y, c = (lax.axis_index(a) for a in AXES)
     group = z * 8 + y * 2 + c
     shift, size = ref["shift"], ref["size"]
@@ -176,8 +179,8 @@
     acc[...] = jnp.zeros_like(acc)
 
     def term_of(k):
-        want = lax.rem(k + 1, 4)
-        t = jnp.int32(0)
+        want = (k + 1) % 4
+        t = 0
         for i in range(1, 4):
             t = jnp.where(shift[group * 4 + i] == want, i, t)
         return t
@@ -197,10 +200,11 @@
         return to("op_2", 1 - c, c_send.at[n], c_recv.at[n], send_sem.at[0], c_sem.at[n])
 
     def state(b, h):
-        cut = WX + WY[h]
+        wx = WX[b]
+        cut = wx + WY[b][h]
         return (
-            lambda *at: rowsb[(b, h, *at, slice(None), slice(0, WX))].astype(F32),
-            lambda *at: rowsb[(b, h, *at, slice(None), slice(WX, cut))].astype(F32),
+            lambda *at: rowsb[(b, h, *at, slice(None), slice(0, wx))].astype(F32),
+            lambda *at: rowsb[(b, h, *at, slice(None), slice(wx, cut))].astype(F32),
             lambda *at: rowsb[(b, h, *at, slice(None), slice(cut, 512))].astype(F32),
         )
 
@@ -209,21 +213,17 @@
     def left_step(p):
         b, k = decode(p)
         t = term_of(k)
-        slot = lax.rem(p, 2)
-        for i in range(2):
-
-            @pl.when(b == i)
-            def _():
-                a = leftb[i][t].reshape(512, 1024)
-                for q in range(4):
-                    cols = slice(q * 256, (q + 1) * 256)
-                    o = jnp.dot(a, psib[:, cols], preferred_element_type=F32).astype(BF)
-                    image0[slot, :, cols] = o[:256]
-                    image1[slot, :, cols] = o[256:]
+        slot = p % 2
+        a = leftb[b][t].reshape(512, 1024)
+        for q in range(4):
+            cols = slice(q * 256, (q + 1) * 256)
+            o = jnp.dot(a, psib[:, cols], preferred_element_type=F32).astype(BF)
+            image0[slot, :, cols] = o[:256]
+            image1[slot, :, cols] = o[256:]
 
     def partner_half(p, halves):
         t = term_of(decode(p)[1])
-        a = image0[lax.rem(p, 2)]
+        a = image0[p % 2]
         for h in halves:
             for q in range(2):
                 cols = slice(q * 256, (q + 1) * 256)
@@ -238,7 +238,7 @@
         t = term_of(k)
         for h in range(2):
             core_copy(p * 2 + h).wait_recv()
-        a = image1[lax.rem(p, 2)]
+        a = image1[p % 2]
         for h in range(2):
             for q in range(2):
                 cols = slice(q * 256, (q + 1) * 256)
@@ -247,52 +247,46 @@
                 for j in range(2):
                     w = v[..., j * 128 : (j + 1) * 128]
                     at = q * 256 + j * 128
-                    if at < WX:
+                    wx = WX[b]
+                    cut = wx + WY[b][h]
+                    if at < wx:
                         for i in range(4):
-                            sx[h][p, i] = w[:, i]
-                    elif at < WX + WY[h]:
+                            sx[h][k, i] = w[:, i]
+                    elif at < cut:
                         for i in range(4):
-                            sy[h][p, i, :, :, at - WX : at - WX + 128] = w[:, i]
+                            sy[b][h][k, i, :, :, at - wx : at - wx + 128] = w[:, i]
                     else:
-                        sz[h][p, :, :, :, at - WX - WY[h] : at - WX - WY[h] + 128] = w
+                        sz[b][h][k, :, :, :, at - cut : at - cut + 128] = w
         for h in range(2):
             n = p * 2 + h
             for d in range(1, 4):
                 yd = ring(y, d)
                 zd = ring(z, d)
-                to("op_1", yd, sy[h].at[p, yd], ry[h].at[p, d - 1], send_sem.at[4 + h], y_sem.at[n]).start()
-                to("op_0", zd, sz[h].at[p, zd], rz[h].at[p, d - 1], send_sem.at[6 + h], z_sem.at[n]).start()
-
-        @pl.when(k < 3)
-        def _():
+                to("op_1", yd, sy[b][h].at[k, yd], ry[b][h].at[k, d - 1], send_sem.at[4 + 2 * b + h], y_sem.at[n]).start()
+                to("op_0", zd, sz[b][h].at[k, zd], rz[b][h].at[k, d - 1], send_sem.at[8 + 2 * b + h], z_sem.at[n]).start()
+
+        if k < 3 and WX[b]:
             for h in range(2):
-                to(
-                    "sec", ring(x, k + 1), sx[h].at[p], rx[h].at[b, k], send_sem.at[2 + h], x_sem.at[b * 2 + h]
-                ).start()
-
-        @pl.when(k == 3)
-        def _():
-            for h in range(2):
-                own_target(p, b, h)
-
-    def own_target(p, b, h):
-        g = b * 2 + h
+                to("sec", ring(x, k + 1), sx[h].at[k], rx[h].at[k], send_sem.at[2 + h], x_sem.at[h]).start()
+
+    def own_target(b, h):
         ox, oy, oz = state(b, h)
-        drain(rx[h].at[b], x_sem.at[g])
         part = jnp.zeros((8, 128), F32)
+        if WX[b]:
+            drain(rx[h], x_sem.at[h])
+            for i in range(4):
+                w = sx[h][3, i].astype(F32)
+                for j in range(3):
+                    w += rx[h][j, i].astype(F32)
+                fx[h][i] = w
+                vx[h][i] = w.astype(BF)
+                part += fold(w * ox(every, i))
+            for d in range(1, 4):
+                yd = ring(y, d)
+                to("op_1", yd, vx[h].at[yd], rvx[h].at[d - 1], send_sem.at[12 + h], vx_sem.at[h]).start()
         for i in range(4):
-            w = sx[h][p, i].astype(F32)
-            for j in range(3):
-                w += rx[h][b, j, i].astype(F32)
-            fx[h][b, i] = w
-            vx[h][b, i] = w.astype(BF)
-            part += fold(w * ox(every, i))
-        for d in range(1, 4):
-            yd = ring(y, d)
-            to("op_1", yd, vx[h].at[b, yd], rvx[h].at[b, d - 1], send_sem.at[8 + h], vx_sem.at[g]).start()
-        for i in range(4):
-            part += fold(sy[h][p, i].astype(F32) * oy(every, i))
-            part += fold(sz[h][p, i].astype(F32) * oz(i, every))
+            part += fold(sy[b][h][3, i].astype(F32) * oy(every, i))
+            part += fold(sz[b][h][3, i].astype(F32) * oz(i, every))
         acc[0:8] += part
 
     def second(p):
@@ -300,24 +294,22 @@
         for h in range(2):
             n = p * 2 + h
             g = b * 2 + h
-            drain(ry[h].at[p], y_sem.at[n])
-            drain(rz[h].at[p], z_sem.at[n])
-            vy = sy[h][p, y].astype(F32)
-            vz = sz[h][p, z].astype(F32)
+            drain(ry[b][h].at[k], y_sem.at[n])
+            drain(rz[b][h].at[k], z_sem.at[n])
+            vy = sy[b][h][k, y].astype(F32)
+            vz = sz[b][h][k, z].astype(F32)
             for d in range(3):
-                vy += ry[h][p, d].astype(F32)
-                vz += rz[h][p, d].astype(F32)
-
-            toy[h][b] = vy
-            toz[h][b] = vz
-
-            @pl.when(k < 3)
-            def _():
-                ty[h][b, k] = vy.astype(BF)
-                tz[h][b, k] = vz.astype(BF)
+                vy += ry[b][h][k, d].astype(F32)
+                vz += rz[b][h][k, d].astype(F32)
+            if k < 3:
+                ty[b][h][k] = vy.astype(BF)
+                tz[b][h][k] = vz.astype(BF)
                 who = ring(x, k + 1)
-                to("sec", who, ty[h].at[b, k], rxy[h].at[b, k], send_sem.at[10 + h], xy_sem.at[g]).start()
-                to("sec", who, tz[h].at[b, k], rxz[h].at[b, k], send_sem.at[12 + h], xz_sem.at[g]).start()
+                to("sec", who, ty[b][h].at[k], rxy[b][h].at[k], send_sem.at[14 + g], xy_sem.at[g]).start()
+                to("sec", who, tz[b][h].at[k], rxz[b][h].at[k], send_sem.at[18 + g], xz_sem.at[g]).start()
+            else:
+                toy[b][h][...] = vy
+                toz[b][h][...] = vz
 
     def cross_share(p):
         b, k = decode(p)
@@ -334,12 +326,12 @@
         live_z = row(64, z * 256) < there
         part = jnp.zeros((8, 128), F32)
         for h in range(2):
-            for i in range(0, WY[h], 128):
+            for i in range(0, WY[1][h], 128):
                 w = othery[h][k, :, :, i : i + 128].astype(F32)
-                part += fold(ty[h][b, k, :, :, i : i + 128].astype(F32) * jnp.where(live_y, w, 0.0))
-            for i in range(0, WZ[h], 128):
+                part += fold(ty[b][h][k, :, :, i : i + 128].astype(F32) * jnp.where(live_y, w, 0.0))
+            for i in range(0, WZ[1][h], 128):
                 w = otherz[h][k, :, :, i : i + 128].astype(F32)
-                part += fold(tz[h][b, k, :, :, i : i + 128].astype(F32) * jnp.where(live_z, w, 0.0))
+                part += fold(tz[b][h][k, :, :, i : i + 128].astype(F32) * jnp.where(live_z, w, 0.0))
         acc[0:8] += part
 
     def mask_rows():
@@ -365,54 +357,52 @@
         cp.wait()
     for cp in right_cp[1:] + left_cp[1] + rows_cp:
         cp.start()
-    left_step(jnp.int32(0))
+    left_step(0)
     pl.semaphore_wait(barrier, 22)
     for k in range(3):
         who = ring(x, 3 - k)
         for h in range(2):
-            cols_y = pl.ds(h * 512 + WX, WY[h])
-            cols_z = pl.ds(h * 512 + WX + WY[h], WZ[h])
+            cols_y = pl.ds(h * 512 + WX[1], WY[1][h])
+            cols_z = pl.ds(h * 512 + WX[1] + WY[1][h], WZ[1][h])
             to("sec", who, psi_rows.at[:, y, c, 1, :, cols_y], othery[h].at[k], other_send.at[h], other_recv.at[h]).start()
             to("sec", who, psi_rows.at[z, :, c, 1, :, cols_z], otherz[h].at[k], other_send.at[2 + h], other_recv.at[2 + h]).start()
     right_cp[0].wait()
-    partner_half(jnp.int32(0), (0,))
-    left_step(jnp.int32(1))
+    partner_half(0, (0,))
+    left_step(1)
     right_cp[1].wait()
-    partner_half(jnp.int32(0), (1,))
+    partner_half(0, (1,))
     mask_rows()
 
-    @pl.loop(1, PAIRS)
-    def _(p):
-        @pl.when(p == 2)
-        def _():
+    for p in range(1, PAIRS):
+        if p == 2:
             for cp in left_cp[1]:
                 cp.wait()
-
         partner_half(p, (0, 1))
         own_half(p - 1)
-
-        @pl.when(p < PAIRS - 1)
-        def _():
+        if p < PAIRS - 1:
             left_step(p + 1)
-
-        @pl.when(p >= LAG)
-        def _():
+        else:
+            for h in range(2):
+                own_target(0, h)
+        if p >= LAG:
             second(p - LAG)
+    own_half(PAIRS - 1)
 
     for h in range(2):
         _, oy, oz = state(0, h)
-        drain(rxy[h].at[0], xy_sem.at[h])
-        drain(rxz[h].at[0], xz_sem.at[h])
-        ay = rxy[h][0, 0].astype(F32) + rxy[h][0, 1].astype(F32) + rxy[h][0, 2].astype(F32)
-        az = rxz[h][0, 0].astype(F32) + rxz[h][0, 1].astype(F32) + rxz[h][0, 2].astype(F32)
+        drain(rxy[0][h], xy_sem.at[h])
+        drain(rxz[0][h], xz_sem.at[h])
+        ay = rxy[0][h][0].astype(F32) + rxy[0][h][1].astype(F32) + rxy[0][h][2].astype(F32)
+        az = rxz[0][h][0].astype(F32) + rxz[0][h][1].astype(F32) + rxz[0][h][2].astype(F32)
         acc[0:8] += fold(ay * oy(every, y)) + fold(az * oz(z, every))
         drain(othery[h], other_recv.at[h])
         drain(otherz[h], other_recv.at[2 + h])
-    cross_share(jnp.int32(3))
-    cross_share(jnp.int32(4))
-    own_half(jnp.int32(PAIRS - 1))
-    second(jnp.int32(5))
-    cross_share(jnp.int32(5))
+    cross_share(3)
+    cross_share(4)
+    for h in range(2):
+        own_target(1, h)
+    second(5)
+    cross_share(5)
     groups = [(b, h) for b in range(2) for h in range(2)]
 
     def reduce_start(stage, dst, devices):
@@ -443,58 +433,63 @@
     reduce_start(0, red_xy, plane)
 
     for b in range(2):
-        second(jnp.int32(PAIRS - 2 + b))
+        second(PAIRS - 2 + b)
         for h in range(2):
             g = b * 2 + h
             if b == 1:
-                drain(rxy[h].at[b], xy_sem.at[g])
-                drain(rxz[h].at[b], xz_sem.at[g])
-            vy = toy[h][b]
-            vz = toz[h][b]
+                drain(rxy[b][h], xy_sem.at[g])
+                drain(rxz[b][h], xz_sem.at[g])
+            vy = toy[b][h][...]
+            vz = toz[b][h][...]
             for d in range(3):
-                vy += rxy[h][b, d].astype(F32)
-                vz += rxz[h][b, d].astype(F32)
-            toy[h][b] = vy
-            toz[h][b] = vz
-            uy[h][b] = vy.astype(BF)
-            uz[h][b] = vz.astype(BF)
+                vy += rxy[b][h][d].astype(F32)
+                vz += rxz[b][h][d].astype(F32)
+            toy[b][h][...] = vy
+            toz[b][h][...] = vz
+            uy[b][h][...] = vy.astype(BF)
+            uz[b][h][...] = vz.astype(BF)
             for d in range(1, 4):
                 zd = ring(z, d)
                 yd = ring(y, d)
-                to("op_0", zd, uy[h].at[b, zd], ruy[h].at[b, d - 1], send_sem.at[14 + h], uy_sem.at[g]).start()
-                to("op_1", yd, uz[h].at[b, yd], ruz[h].at[b, d - 1], send_sem.at[16 + h], uz_sem.at[g]).start()
-            drain(rvx[h].at[b], vx_sem.at[g])
-            v = fx[h][b, y]
-            for d in range(3):
-                v += rvx[h][b, d].astype(F32)
-            gx[h][b] = v
-            ux[h][b] = v.astype(BF)
-            for d in range(1, 4):
-                zd = ring(z, d)
-                to("op_0", zd, ux[h].at[b, zd], rux[h].at[b, d - 1], send_sem.at[18 + h], ux_sem.at[g]).start()
+                to("op_0", zd, uy[b][h].at[zd], ruy[b][h].at[d - 1], send_sem.at[22 + g], uy_sem.at[g]).start()
+                to("op_1", yd, uz[b][h].at[yd], ruz[b][h].at[d - 1], send_sem.at[26 + g], uz_sem.at[g]).start()
+            if WX[b]:
+                drain(rvx[h], vx_sem.at[h])
+                v = fx[h][y]
+                for d in range(3):
+                    v += rvx[h][d].astype(F32)
+                gx[h][...] = v
+                ux[h][...] = v.astype(BF)
+                for d in range(1, 4):
+                    zd = ring(z, d)
+                    to("op_0", zd, ux[h].at[zd], rux[h].at[d - 1], send_sem.at[30 + h], ux_sem.at[h]).start()
     red[1] = reduce_finish(0, red_xy, 15)
     stack = [{"op_0": ring(z, i // 2), "op_2": lax.rem(c + i % 2, 2)} for i in range(1, 8)]
     reduce_start(1, red_zc, stack)
     for b, h in groups:
         g = b * 2 + h
-        drain(ruy[h].at[b], uy_sem.at[g])
-        drain(ruz[h].at[b], uz_sem.at[g])
-        drain(rux[h].at[b], ux_sem.at[g])
-        v = gx[h][b, z]
-        vy = toy[h][b, z]
-        vz = toz[h][b, y]
+        drain(ruy[b][h], uy_sem.at[g])
+        drain(ruz[b][h], uz_sem.at[g])
+        vy = toy[b][h][z]
+        vz = toz[b][h][y]
         for d in range(3):
-            v += rux[h][b, d].astype(F32)
-            vy += ruy[h][b, d].astype(F32)
-            vz += ruz[h][b, d].astype(F32)
+            vy += ruy[b][h][d].astype(F32)
+            vz += ruz[b][h][d].astype(F32)
+        parts = [vy, vz]
+        if WX[b]:
+            drain(rux[h], ux_sem.at[h])
+            v = gx[h][z]
+            for d in range(3):
+                v += rux[h][d].astype(F32)
+            parts = [v] + parts
         first = z * 256 + y * 64 + c * 32 + b * 16
         rows = slice(b * 16, b * 16 + 16)
         at = h * 512
-        cut = at + WX + WY[h]
-        keep = (first + lax.broadcasted_iota(jnp.int32, (16, 512), 0)) < live
-        sig[rows, at : at + WX] = jnp.where(keep[:, :WX], v, 0.0)
-        sig[rows, at + WX : cut] = jnp.where(keep[:, WX : WX + WY[h]], vy, 0.0)
-        sig[rows, cut : at + 512] = jnp.where(keep[:, WX + WY[h] :], vz, 0.0)
+        for v in parts:
+            wide = v.shape[-1]
+            keep = (first + lax.broadcasted_iota(jnp.int32, v.shape, 0)) < live
+            sig[rows, at : at + wide] = jnp.where(keep, v, 0.0)
+            at += wide
     sig_cp = pltpu.make_async_copy(sig, sig_out, load_sem.at[0])
     sig_cp.start()
     total = reduce_finish(1, red_zc, 7)
@@ -507,8 +502,17 @@
     for h in range(2):
         drain(othery[h], other_send.at[h])
         drain(otherz[h], other_send.at[2 + h])
-        for i, buf in enumerate((rx, ry, rz, rvx, rxy, rxz, ruy, ruz, rux)):
-            drain(buf[h], send_sem.at[2 + 2 * i + h])
+        drain(rx[h], send_sem.at[2 + h])
+        drain(rvx[h], send_sem.at[12 + h])
+        drain(rux[h], send_sem.at[30 + h])
+        for b in range(2):
+            g = b * 2 + h
+            drain(ry[b][h], send_sem.at[4 + g])
+            drain(rz[b][h], send_sem.at[8 + g])
+            drain(rxy[b][h], send_sem.at[14 + g])
+            drain(rxz[b][h], send_sem.at[18 + g])
+            drain(ruy[b][h], send_sem.at[22 + g])
+            drain(ruz[b][h], send_sem.at[26 + g])
     drain(red_xy, red_send.at[0])
     drain(red_zc, red_send.at[1])
     for cp in state_cp + [sig_cp, energy_cp]:

time: 50.9 us -> 48.3 us (0.949)
  Pallas kernels: 48.5 us -> 45.9 us
    pallas_call x1, Pallas kernels: 48.5 us -> 45.9 us  [per_device(): pl.pallas_call(kernel, out_shape=(out, jax.ShapeDtypeStruct((32, 1024), B...]
where the time goes in v3:
time: 48.3 us; the launch traced here: 48.2 us
  Pallas kernels  45.9 us (95%)
  other arithmetic  1.63 us (3%)
  between operations  0.64 us (1%)
    pallas_call x1, Pallas kernels, per_device(): pl.pallas_call(kernel, out_shape=(out, jax.ShapeDtypeStruct((32, 1024), B...  45.9 us
    broadcast_in_dim x1, other arithmetic, per_device(): return (sigma[None], (sigma - energy * state.astype(F32))[None])  1.63 us

profile of v3, /device:TPU:1, one launch (start us, length us, event | category | flops | bytes accessed | tf_op | source)
XLA Modules:
  0.0 48.2 jit_solution(13805333955311864310)
XLA Ops:
  0.6 45.9 %sigma_step.1 = (f32[32,1024]{1,0:T(8,128)}, bf16[32,1024]{1,0:T(8,128)(2,1)}, f32[1,1024]{1,0:T(1,128)}, f32[1,1024]{1,0:T(1,128)}) custom-call(s32[128]{0:T(128)} %shift_in.1, s32[4]{0:T(128)} %size_in.1, bf16[1024,1024]{1,0:T(8,128)(2,1)} %bitcast.10, bf16[4,4,2,2,16,1024]{5,4,3,2,1,0:T(8,128)(2,1)} %bitcast.11, ...), custom_call_target="tpu_custom_call" | custom-call | tf_op jit(solution)/shard_map/sigma_step/pallas_call | solution.py:527
  46.5 1.6 %subtract_bitcast_fusion = (f32[1,32,1024]{2,1,0:T(8,128)}, f32[1,32,1024]{2,1,0:T(8,128)}) fusion(bf16[32,1024]{1,0:T(8,128)(2,1)} %get-tuple-element.9, f32[32,1024]{1,0:T(8,128)} %get-tuple-element.6, f32[1024]{0:T(1024)} %bitcast.12, f32[1024]{0:T(1024)} %bitcast.13), kind=kLoop, calls=%fused_computation | loop fusion | flops 131072 | bytes 466944 | tf_op jit(solution)/shard_map/broadcast_in_dim | solution.py:546

commit v4 on v3

--- a/solution.py
+++ b/solution.py
@@ -233,13 +233,13 @@
         for h in halves:
             core_copy(p * 2 + h).start()
 
-    def own_half(p):
+    def own_half(p, halves):
         b, k = decode(p)
         t = term_of(k)
-        for h in range(2):
+        for h in halves:
             core_copy(p * 2 + h).wait_recv()
         a = image1[p % 2]
-        for h in range(2):
+        for h in halves:
             for q in range(2):
                 cols = slice(q * 256, (q + 1) * 256)
                 v = jnp.dot(a, rightb[h][t, :, cols], preferred_element_type=F32).astype(BF).astype(F32)
@@ -257,7 +257,7 @@
                             sy[b][h][k, i, :, :, at - wx : at - wx + 128] = w[:, i]
                     else:
                         sz[b][h][k, :, :, :, at - cut : at - cut + 128] = w
-        for h in range(2):
+        for h in halves:
             n = p * 2 + h
             for d in range(1, 4):
                 yd = ring(y, d)
@@ -266,7 +266,7 @@
                 to("op_0", zd, sz[b][h].at[k, zd], rz[b][h].at[k, d - 1], send_sem.at[8 + 2 * b + h], z_sem.at[n]).start()
 
         if k < 3 and WX[b]:
-            for h in range(2):
+            for h in halves:
                 to("sec", ring(x, k + 1), sx[h].at[k], rx[h].at[k], send_sem.at[2 + h], x_sem.at[h]).start()
 
     def own_target(b, h):
@@ -377,8 +377,9 @@
         if p == 2:
             for cp in left_cp[1]:
                 cp.wait()
-        partner_half(p, (0, 1))
-        own_half(p - 1)
+        for halves in ((0, 1),) if p < PAIRS - 1 else ((0,), (1,)):
+            partner_half(p, halves)
+        own_half(p - 1, (0, 1))
         if p < PAIRS - 1:
             left_step(p + 1)
         else:
@@ -386,7 +387,8 @@
                 own_target(0, h)
         if p >= LAG:
             second(p - LAG)
-    own_half(PAIRS - 1)
+    own_half(PAIRS - 1, (0,))
+    own_half(PAIRS - 1, (1,))
 
     for h in range(2):
         _, oy, oz = state(0, h)

time: 48.3 us -> 48.5 us (level)
  no operation moved by 1% of the time
where the time goes in v4:
time: 48.5 us; the launch traced here: 48.4 us
  Pallas kernels  46.1 us (95%)
  other arithmetic  1.63 us (3%)
  between operations  0.64 us (1%)
    pallas_call x1, Pallas kernels, per_device(): pl.pallas_call(kernel, out_shape=(out, jax.ShapeDtypeStruct((32, 1024), B...  46.1 us
    broadcast_in_dim x1, other arithmetic, per_device(): return (sigma[None], (sigma - energy * state.astype(F32))[None])  1.63 us

profile of v4, /device:TPU:1, one launch (start us, length us, event | category | flops | bytes accessed | tf_op | source)
XLA Modules:
  0.0 48.4 jit_solution(16066871212003769185)
XLA Ops:
  0.6 46.1 %sigma_step.1 = (f32[32,1024]{1,0:T(8,128)}, bf16[32,1024]{1,0:T(8,128)(2,1)}, f32[1,1024]{1,0:T(1,128)}, f32[1,1024]{1,0:T(1,128)}) custom-call(s32[128]{0:T(128)} %shift_in.1, s32[4]{0:T(128)} %size_in.1, bf16[1024,1024]{1,0:T(8,128)(2,1)} %bitcast.10, bf16[4,4,2,2,16,1024]{5,4,3,2,1,0:T(8,128)(2,1)} %bitcast.11, ...), custom_call_target="tpu_custom_call" | custom-call | tf_op jit(solution)/shard_map/sigma_step/pallas_call | solution.py:529
  46.7 1.6 %subtract_bitcast_fusion = (f32[1,32,1024]{2,1,0:T(8,128)}, f32[1,32,1024]{2,1,0:T(8,128)}) fusion(bf16[32,1024]{1,0:T(8,128)(2,1)} %get-tuple-element.9, f32[32,1024]{1,0:T(8,128)} %get-tuple-element.6, f32[1024]{0:T(1024)} %bitcast.12, f32[1024]{0:T(1024)} %bitcast.13), kind=kLoop, calls=%fused_computation | loop fusion | flops 131072 | bytes 466944 | tf_op jit(solution)/shard_map/broadcast_in_dim | solution.py:548
